TPU v7x, 256 devices: a whole 4x4x8 slice. The times are simulated.
256 devices in a mesh: grp: 8 (over y, core), row: 32 (over z, x).
Axes of the slice: x: 4, y: 4, z: 8, core: 2. Of those that a mesh axis runs over, the one named last changes fastest.
Arguments:
- features: bfloat16 [524288, 256], P(('grp', 'row')), may hold values from -6 to 6
- cotangent: bfloat16 [524288, 256], P(('grp', 'row')), may hold values from -6 to 6
- self_weight: bfloat16 [256, 256], replicated, may hold values from -0.375 to 0.375
- neighbor_weight: bfloat16 [256, 256], replicated, may hold values from -0.375 to 0.375
- tile_values: bfloat16 [256, 64, 128, 128], P(('grp', 'row')), may hold values from 0 to 1
- tile_index: int32 [256, 64, 2], P(('grp', 'row')), may hold values from 0 to 15
- hub_adjacency: bfloat16 [524288, 1024], P(('grp', 'row')), may hold values from 0 to 1
- hub_owner: int32 [8, 8], P('grp'), may hold values from 0 to 31
- send_rows: int32 [256, 8, 64], P(('grp', 'row')), may hold values from 0 to 2047
- cut_adjacency: bfloat16 [524288, 512], P(('grp', 'row')), may hold values from 0 to 1
- degrees: int32 [524288], P(('grp', 'row')), may hold values from 1024 to 2047
Outputs:
- hidden: bfloat16 [524288, 256], P(('grp', 'row'))
- grad_features: bfloat16 [524288, 256], P(('grp', 'row'))
- grad_self: float32 [256, 256], replicated
- grad_neighbor: float32 [256, 256], replicated
Inputs may be any that keep to these rules, and one draw needn't show every extreme that they name: `send_rows`: rows may repeat.
All inputs are finite; a program needn't handle non-finite values.
Results may differ from a plain program's by a relative error of at most 0.014.
Values may be sent and summed in bfloat16 or wider, within the bound.
A program may use at most 128 MiB of HBM per device.

v0:
```python
import jax
import jax.numpy as jnp
from jax import lax
from jax.sharding import PartitionSpec as P

TILE = 128
HUB = 128


def spread(value, axis, root):
    mine = lax.axis_index(axis) == root
    return lax.psum(jnp.where(mine, value, jnp.zeros_like(value)), axis)


def on_device(
    features,
    cotangent,
    self_weight,
    neighbor_weight,
    tile_values,
    tile_index,
    hub_adjacency,
    hub_owner,
    send_rows,
    cut_adjacency,
    degrees,
):
    node_count, width = features.shape
    tile_total = node_count // TILE
    group_count = lax.axis_size("grp")
    section_count = hub_owner.shape[1]
    values = tile_values[0]
    index = tile_index[0]
    owners = hub_owner[0]
    blocks = features.reshape(tile_total, TILE, width)
    row_select = (index[:, 0][None, :] == jnp.arange(tile_total)[:, None]).astype(jnp.float32)
    col_select = (index[:, 1][None, :] == jnp.arange(tile_total)[:, None]).astype(jnp.float32)
    picked = blocks[index[:, 1]]
    product = jnp.einsum("lab,lbf->laf", values, picked, preferred_element_type=jnp.float32)
    local_sum = jnp.einsum(
        "nl,laf->naf", row_select, product, precision=lax.Precision.HIGHEST
    ).reshape(node_count, width)
    heads = features[:HUB]
    hub_sum = jnp.zeros((node_count, width), jnp.float32)
    for section in range(section_count):
        panel = spread(heads, "row", owners[section])
        hub_sum = hub_sum + jnp.dot(
            hub_adjacency[:, section * HUB : (section + 1) * HUB],
            panel,
            preferred_element_type=jnp.float32,
        )
    outgoing = features[send_rows[0]]
    arrived = lax.all_to_all(outgoing, "grp", split_axis=0, concat_axis=0, tiled=True)
    cut_sum = jnp.dot(
        cut_adjacency,
        arrived.reshape(group_count * outgoing.shape[1], width),
        preferred_element_type=jnp.float32,
    )
    scaling = lax.rsqrt(degrees.astype(jnp.float32))[:, None]
    aggregated = ((local_sum + hub_sum + cut_sum) * scaling).astype(jnp.bfloat16)
    before = jnp.dot(features, self_weight, preferred_element_type=jnp.float32) + jnp.dot(
        aggregated, neighbor_weight, preferred_element_type=jnp.float32
    )
    activated, pullback = jax.vjp(jax.nn.gelu, before)
    hidden = activated.astype(jnp.bfloat16)
    grad_before = pullback(cotangent.astype(jnp.float32))[0].astype(jnp.bfloat16)
    rows_dims = (((0,), (0,)), ((), ()))
    cols_dims = (((1,), (1,)), ((), ()))
    self_part = lax.dot_general(
        features, grad_before, rows_dims, preferred_element_type=jnp.float32
    )
    neighbor_part = lax.dot_general(
        aggregated, grad_before, rows_dims, preferred_element_type=jnp.float32
    )
    grad_self, grad_neighbor = lax.psum((self_part, neighbor_part), ("grp", "row"))
    grad_aggregate = (
        lax.dot_general(grad_before, neighbor_weight, cols_dims, preferred_element_type=jnp.float32)
        * scaling
    ).astype(jnp.bfloat16)
    grad_total = lax.dot_general(
        grad_before, self_weight, cols_dims, preferred_element_type=jnp.float32
    )
    agg_blocks = grad_aggregate.reshape(tile_total, TILE, width)[index[:, 0]]
    returned = jnp.einsum("lab,laf->lbf", values, agg_blocks, preferred_element_type=jnp.float32)
    grad_total = grad_total + jnp.einsum(
        "nl,lbf->nbf", col_select, returned, precision=lax.Precision.HIGHEST
    ).reshape(node_count, width)
    hub_terms = lax.dot_general(
        hub_adjacency, grad_aggregate, rows_dims, preferred_element_type=jnp.float32
    ).reshape(section_count, HUB, width)
    totals = lax.psum(hub_terms.astype(jnp.bfloat16), "row").astype(jnp.float32)
    owned = (owners == lax.axis_index("row")).astype(jnp.float32)
    hub_grad = jnp.einsum("s,shf->hf", owned, totals, precision=lax.Precision.HIGHEST)
    grad_total = grad_total.at[:HUB].add(hub_grad)
    back_rows = lax.dot_general(
        cut_adjacency, grad_aggregate, rows_dims, preferred_element_type=jnp.float32
    ).astype(jnp.bfloat16)
    back_rows = back_rows.reshape(group_count, -1, width)
    returned_rows = lax.all_to_all(back_rows, "grp", split_axis=0, concat_axis=0, tiled=True)
    scatter_table = (send_rows[0].reshape(-1)[None, :] == jnp.arange(node_count)[:, None]).astype(
        jnp.bfloat16
    )
    grad_total = grad_total + jnp.dot(
        scatter_table, returned_rows.reshape(-1, width), preferred_element_type=jnp.float32
    )
    return (hidden, grad_total.astype(jnp.bfloat16), grad_self, grad_neighbor)


def solution(mesh):
    in_specs = (
        P(("grp", "row"), None),
        P(("grp", "row"), None),
        P(),
        P(),
        P(("grp", "row"), None, None, None),
        P(("grp", "row"), None, None),
        P(("grp", "row"), None),
        P("grp", None),
        P(("grp", "row"), None, None),
        P(("grp", "row"), None),
        P(("grp", "row")),
    )
    out_specs = (P(("grp", "row"), None), P(("grp", "row"), None), P(), P())
    return jax.shard_map(
        on_device, mesh=mesh, in_specs=in_specs, out_specs=out_specs, check_vma=False
    )
```

profile of v0, /device:TPU:8, one launch (start us, length us, event | category | flops | bytes accessed | tf_op | source)
XLA Modules:
  0.0 638.3 jit_solution(11707294678581093016)
XLA Ops:
  8.2 3.6 gather_fusion.1
  11.7 5.5 all-to-all-start
  25.0 2.8 gather_fusion
  27.8 6.8 %fusion.25 = f32[64,256,128]{2,1,0:T(8,128)} fusion(bf16[64,128,256]{2,1,0:T(8,128)(2,1)} %gather_fusion, bf16[1,64,128,128]{3,2,1,0:T(8,128)(2,1)S(1)} %copy-done), kind=kOutput, calls=%fused_computation.44 | convolution fusion | flops 536870912 | bytes 14680064 | tf_op jit(solution)/shard_map/lab,lbf->laf/dot_general | solution.py:39
  34.6 9.2 %copy.25 = f32[64,256,128]{1,0,2:T(8,128)} copy(f32[64,256,128]{2,1,0:T(8,128)} %fusion.25) | data formatting | bytes 16777216 | tf_op jit(solution)/shard_map/lab,lbf->laf/dot_general | solution.py:39
  43.8 5.2 fusion.2
  48.9 2.6 copy.18
  51.5 2.9 copy.19
  57.0 117.7 %all-reduce.10.cloned.1.call-done = (bf16[128,256]{1,0:T(8,128)(2,1)}, bf16[128,256]{1,0:T(8,128)(2,1)}, bf16[128,256]{1,0:T(8,128)(2,1)}, bf16[128,256]{1,0:T(8...) async-done(((bf16[128,256]{1,0:T(8,128)(2,1)}, bf16[128,256]{1,0:T(8,128)(2,1)}, ...) | async-done | bytes 524304 | tf_op jit(solution)/shard_map/psum | solution.py:12
  185.4 3.1 fusion.10
  188.5 3.0 fusion.15
  193.9 2.7 fusion.12
  198.2 2.8 gather_fusion.2
  201.0 6.8 %fusion.23 = f32[64,256,128]{2,1,0:T(8,128)} fusion(bf16[64,128,256]{2,1,0:T(8,128)(2,1)} %gather_fusion.2, bf16[1,64,128,128]{3,2,1,0:T(8,128)(2,1)S(1)} %copy-done), kind=kOutput, calls=%fused_computation.42 | convolution fusion | flops 536870912 | bytes 14680064 | tf_op jit(solution)/shard_map/lab,laf->lbf/dot_general | solution.py:84
  207.8 9.2 %copy.27 = f32[64,256,128]{1,0,2:T(8,128)} copy(f32[64,256,128]{2,1,0:T(8,128)} %fusion.23) | data formatting | bytes 16777216 | tf_op jit(solution)/shard_map/lab,laf->lbf/dot_general | solution.py:84
  217.0 5.2 fusion
  222.2 2.6 copy.22
  224.8 3.4 fusion.28
  229.2 2.7 fusion.29
  232.8 4.8 all-to-all-start.1
  237.6 3.4 convolution_add_fusion
  241.0 233.6 %all-reduce.8.cloned.1.call-done = (f32[256,256]{0,1:T(8,128)}, f32[256,256]{1,0:T(8,128)}) async-done(((f32[256,256]{0,1:T(8,128)}, f32[256,256]{1,0:T(8,128)}), (f32[256,256]{0,1:T(8,128)}, f32[256,256]{1,0:T(8,128)})) %all-reduce.8.cloned.1.call-update) | async-done | bytes 524304 | tf_op jit(solution)/shard_map/psum | solution.py:75
  476.4 148.1 %all-reduce.6.cloned.1.call-done = bf16[8,128,256]{1,0,2:T(8,128)(2,1)} async-done(((bf16[8,128,256]{1,0,2:T(8,128)(2,1)}), bf16[8,128,256]{1,0,2:T(8,128)(2,1)}) %all-reduce.6.cloned.1.call-update) | async-done | bytes 524304 | tf_op jit(solution)/shard_map/psum | solution.py:91
  627.6 3.4 fusion.11
  (86 shorter events, 28.2 us)
Async XLA Ops:
  7.2 20.6 %copy-start = (bf16[1,64,128,128]{3,2,1,0:T(8,128)(2,1)S(1)}, bf16[1,64,128,128]{3,2,1,0:T(8,128)(2,1)}, u32[]{:S(2)}) copy-start(bf16[1,64,128,128]{3,2,1,0:T(8,128)(2,1)} %param.17) | copy-start | bytes 6291460
  7.2 16.6 %copy-start.20 = (s32[1,8,64]{2,1,0:T(8,128)S(1)}, s32[1,8,64]{2,1,0:T(8,128)}, u32[]{:S(2)}) copy-start(s32[1,8,64]{2,1,0:T(8,128)} %param.21) | copy-start | bytes 6148
  7.2 15.7 %copy-start.1 = (bf16[2048,256]{1,0:T(8,128)(2,1)S(1)}, bf16[2048,256]{1,0:T(8,128)(2,1)}, u32[]{:S(2)}) copy-start(bf16[2048,256]{1,0:T(8,128)(2,1)} %param.13) | copy-start | bytes 3145732
  7.2 10.0 %copy-start.19 = (s32[1,8]{1,0:T(1,128)S(1)}, s32[1,8]{1,0:T(1,128)}, u32[]{:S(2)}) copy-start(s32[1,8]{1,0:T(1,128)} %param.20) | copy-start | bytes 100
  7.2 17.2 %copy-start.23 = (s32[1,64,2]{1,2,0:T(2,128)S(1)}, s32[1,64,2]{1,2,0:T(2,128)}, u32[]{:S(2)}) copy-start(s32[1,64,2]{1,2,0:T(2,128)} %param.18) | copy-start | bytes 1540
  11.7 173.6 %all-to-all-start = ((bf16[8,64,256]{2,1,0:T(8,128)(2,1)}), bf16[8,64,256]{2,1,0:T(8,128)(2,1)S(1)}, u32[]{:S(2)}, u32[]{:S(2)}) async-start(bf16[8,64,256]{2,1,0:T(8,128)(2,1)} %bitcast.18), calls=%async_computation | async-start | bytes 524288 | tf_op jit(solution)/shard_map/all_to_all | solution.py:53
  17.2 157.4 %all-reduce.10.cloned.1.call-start = ((), (), s32[]{:S(2)}) async-start(), calls=%async_computation.4 | async-start | bytes 1048576 | tf_op jit(solution)/shard_map/psum | solution.py:12
  23.7 450.9 %all-reduce.8.cloned.1.call-start = ((), (), s32[]{:S(2)}) async-start(), calls=%async_computation.3 | async-start | bytes 1048576 | tf_op jit(solution)/shard_map/psum | solution.py:75
  51.5 3.6 copy-start.8
  176.2 2.4 copy-start.5
  176.2 2.4 copy-start.17
  182.0 1.6 copy-start.4
  182.0 1.6 copy-start.12
  185.3 3.2 copy-start.7
  185.4 3.2 copy-start.10
  185.4 3.2 copy-start.24
  191.5 2.3 copy-start.11
  207.8 9.2 %copy-start.22 = (s32[64]{0:T(128)S(1)}, s32[64]{0:T(128)}, u32[]{:S(2)}) copy-start(s32[64]{0:T(128)} %get-tuple-element.44) | copy-start | bytes 772
  222.2 2.7 copy-start.6
  224.8 399.8 %all-reduce.6.cloned.1.call-start = ((), (), s32[]{:S(2)}) async-start(), calls=%async_computation.2 | async-start | bytes 1048576 | tf_op jit(solution)/shard_map/psum | solution.py:91
  229.2 8.4 %copy-start.3 = (bf16[2048,256]{1,0:T(8,128)(2,1)S(1)}, bf16[2048,256]{1,0:T(8,128)(2,1)}, u32[]{:S(2)}) copy-start(bf16[2048,256]{1,0:T(8,128)(2,1)} %copy-done.2) | copy-start | bytes 3145732
  232.8 394.9 %all-to-all-start.1 = ((bf16[8,64,256]{2,1,0:T(8,128)(2,1)}), bf16[8,64,256]{2,1,0:T(8,128)(2,1)S(1)}, u32[]{:S(2)}, u32[]{:S(2)}) async-start(bf16[8,64,256]{2,1,0:T(8,128)(2,1)} %bitcast.32), calls=%async_computation.1 | async-start | bytes 524288 | tf_op jit(solution)/shard_map/all_to_all | solution.py:99
  237.6 390.0 %copy-start.21 = (s32[512]{0:T(512)S(1)}, s32[512]{0:T(512)}, u32[]{:S(2)}) copy-start(s32[512]{0:T(512)} %eq.97) | copy-start | bytes 6148
  626.0 5.1 copy-start.9
  (6 other events, 6.1 us)
Sparse Core Ops, SparseCore 0:
  23.8 150.7 all-reduce.9
  224.9 249.6 all-reduce.7
  478.4 146.1 all-reduce.5
where the time goes:
time: 640 us; the launch traced here: 638 us
  waiting for transfers between devices  499 us (78%)
  matrix products  58.4 us (9%)
  local copies, waits for them, and re-layouts  46.5 us (7%)
  between operations  19 us (3%)
  starting transfers between devices  10.4 us (2%)
    psum x1, waiting for transfers between devices, on_device(): lax.psum((self_part, neighbor_part), ('grp', 'row'))  234 us
    psum x1, waiting for transfers between devices, on_device(): totals = lax.psum(hub_terms.astype(jnp.bfloat16), 'row').astype(jnp.float32)  148 us
    psum x1, waiting for transfers between devices, spread(): return lax.psum(jnp.where(mine, value, jnp.zeros_like(value)), axis)  118 us
  transfers between devices with their start and end apart: 5, of which 3 were waited for; matrix products, arithmetic and copies ran while one was open for 9% of the time, Pallas kernels for 0%

commit v1 on v0

--- a/solution.py
+++ b/solution.py
@@ -9,7 +9,7 @@
 
 def spread(value, axis, root):
     mine = lax.axis_index(axis) == root
-    return lax.psum(jnp.where(mine, value, jnp.zeros_like(value)), axis)
+    return jnp.sum(lax.all_gather(jnp.where(mine, value, jnp.zeros_like(value)), axis), axis=0)
 
 
 def on_device(

time: 640 us -> 1110 us (1.73)
  waiting for transfers between devices: 499 us -> 948 us
  other arithmetic: 4.54 us -> 25.3 us
    all_gather x0 -> x8, waiting for transfers between devices: none -> 562 us  [spread(): lax.all_gather(jnp.where(mine, value, jnp.zeros_like(value)), axis)]
    psum x1 -> x0, waiting for transfers between devices: 118 us -> none  [spread(): return lax.psum(jnp.where(mine, value, jnp.zeros_like(value)), axis)]
    reduce_sum x0 -> x8, other arithmetic: none -> 20.1 us  [spread(): jnp.sum(lax.all_gather(jnp.where(mine, value, jnp.zeros_like(value)), axi...]
  transfers between devices with their start and end apart: 5 -> 12, of which waited for: 3 -> 10; matrix products, arithmetic and copies ran while one was open for 9% -> 7% of each run, Pallas kernels for 0% -> 0%
where the time goes in v1:
time: 1110 us
  waiting for transfers between devices  948 us (85%)
  matrix products  58.4 us (5%)
  local copies, waits for them, and re-layouts  46.5 us (4%)
  other arithmetic  25.3 us (2%)
  between operations  19.5 us (2%)
    all_gather x8, waiting for transfers between devices, spread(): lax.all_gather(jnp.where(mine, value, jnp.zeros_like(value)), axis)  562 us
    psum x1, waiting for transfers between devices, on_device(): lax.psum((self_part, neighbor_part), ('grp', 'row'))  234 us
    psum x1, waiting for transfers between devices, on_device(): totals = lax.psum(hub_terms.astype(jnp.bfloat16), 'row').astype(jnp.float32)  148 us
  transfers between devices with their start and end apart: 12, of which 10 were waited for; matrix products, arithmetic and copies ran while one was open for 7% of the time, Pallas kernels for 0%

profile of v1, /device:TPU:8, one launch (start us, length us, event | category | flops | bytes accessed | tf_op | source)
XLA Modules:
  0.0 1108.1 jit_solution(2156423151268111163)
XLA Ops:
  23.7 5.5 all-to-all-start
  33.8 6.8 fusion.25
  40.6 9.2 copy.25
  49.8 5.2 fusion.2
  57.5 2.9 copy.19
  62.3 34.2 %all-gather.17.cloned.1.call-done = bf16[4096,256]{1,0:T(8,128)(2,1)} async-done(((bf16[128,256]{1,0:T(8,128)(2,1)}), bf16[4096,256]{1,0:T(8,128)(2,1)}) %all-gather.17.cloned.1.call-update) | async-done | bytes 2097168 | tf_op jit(solution)/shard_map/all_gather | solution.py:12
  99.0 75.8 %all-gather.19.cloned.1.call-done = bf16[4096,256]{1,0:T(8,128)(2,1)} async-done(((bf16[128,256]{1,0:T(8,128)(2,1)}), bf16[4096,256]{1,0:T(8,128)(2,1)}) %all-gather.19.cloned.1.call-update) | async-done | bytes 2097168 | tf_op jit(solution)/shard_map/all_gather | solution.py:12
  177.3 75.8 %all-gather.21.cloned.1.call-done = bf16[4096,256]{1,0:T(8,128)(2,1)} async-done(((bf16[128,256]{1,0:T(8,128)(2,1)}), bf16[4096,256]{1,0:T(8,128)(2,1)}) %all-gather.21.cloned.1.call-update) | async-done | bytes 2097168 | tf_op jit(solution)/shard_map/all_gather | solution.py:12
  255.7 75.1 %all-gather.23.cloned.1.call-done = bf16[4096,256]{1,0:T(8,128)(2,1)} async-done(((bf16[128,256]{1,0:T(8,128)(2,1)}), bf16[4096,256]{1,0:T(8,128)(2,1)}) %all-gather.23.cloned.1.call-update) | async-done | bytes 2097168 | tf_op jit(solution)/shard_map/all_gather | solution.py:12
  333.2 75.1 %all-gather.25.cloned.1.call-done = bf16[4096,256]{1,0:T(8,128)(2,1)} async-done(((bf16[128,256]{1,0:T(8,128)(2,1)}), bf16[4096,256]{1,0:T(8,128)(2,1)}) %all-gather.25.cloned.1.call-update) | async-done | bytes 2097168 | tf_op jit(solution)/shard_map/all_gather | solution.py:12
  410.8 75.1 %all-gather.27.cloned.1.call-done = bf16[4096,256]{1,0:T(8,128)(2,1)} async-done(((bf16[128,256]{1,0:T(8,128)(2,1)}), bf16[4096,256]{1,0:T(8,128)(2,1)}) %all-gather.27.cloned.1.call-update) | async-done | bytes 2097168 | tf_op jit(solution)/shard_map/all_gather | solution.py:12
  488.4 75.2 %all-gather.29.cloned.1.call-done = bf16[4096,256]{1,0:T(8,128)(2,1)} async-done(((bf16[128,256]{1,0:T(8,128)(2,1)}), bf16[4096,256]{1,0:T(8,128)(2,1)}) %all-gather.29.cloned.1.call-update) | async-done | bytes 2097168 | tf_op jit(solution)/shard_map/all_gather | solution.py:12
  566.1 75.8 %all-gather.31.cloned.1.call-done = bf16[4096,256]{1,0:T(8,128)(2,1)} async-done(((bf16[128,256]{1,0:T(8,128)(2,1)}), bf16[4096,256]{1,0:T(8,128)(2,1)}) %all-gather.31.cloned.1.call-update) | async-done | bytes 2097168 | tf_op jit(solution)/shard_map/all_gather | solution.py:12
  655.2 3.1 fusion.10
  658.4 3.0 fusion.15
  671.0 6.8 fusion.23
  677.8 9.2 copy.27
  686.9 5.2 fusion
  694.8 3.4 fusion.28
  702.7 4.8 all-to-all-start.1
  707.6 3.4 convolution_add_fusion
  711.0 233.7 %all-reduce.6.cloned.1.call-done = (f32[256,256]{0,1:T(8,128)}, f32[256,256]{1,0:T(8,128)}) async-done(((f32[256,256]{0,1:T(8,128)}, f32[256,256]{1,0:T(8,128)}), (f32[256,256]{0,1:T(8,128)}, f32[256,256]{1,0:T(8,128)})) %all-reduce.6.cloned.1.call-update) | async-done | bytes 524304 | tf_op jit(solution)/shard_map/psum | solution.py:75
  946.5 147.6 %all-reduce.4.cloned.1.call-done = bf16[8,128,256]{1,0,2:T(8,128)(2,1)} async-done(((bf16[8,128,256]{1,0,2:T(8,128)(2,1)}), bf16[8,128,256]{1,0,2:T(8,128)(2,1)}) %all-reduce.4.cloned.1.call-update) | async-done | bytes 524304 | tf_op jit(solution)/shard_map/psum | solution.py:91
  1097.1 3.4 fusion.11
  (117 shorter events, 73.3 us)
Async XLA Ops:
  7.2 26.7 %copy-start = (bf16[1,64,128,128]{3,2,1,0:T(8,128)(2,1)S(1)}, bf16[1,64,128,128]{3,2,1,0:T(8,128)(2,1)}, u32[]{:S(2)}) copy-start(bf16[1,64,128,128]{3,2,1,0:T(8,128)(2,1)} %param.17) | copy-start | bytes 6291460
  7.2 13.9 %copy-start.1 = (bf16[2048,256]{1,0:T(8,128)(2,1)S(1)}, bf16[2048,256]{1,0:T(8,128)(2,1)}, u32[]{:S(2)}) copy-start(bf16[2048,256]{1,0:T(8,128)(2,1)} %param.13) | copy-start | bytes 3145732
  7.2 22.0 %copy-start.20 = (s32[1,8,64]{2,1,0:T(8,128)S(1)}, s32[1,8,64]{2,1,0:T(8,128)}, u32[]{:S(2)}) copy-start(s32[1,8,64]{2,1,0:T(8,128)} %param.21) | copy-start | bytes 6148
  7.2 22.6 %copy-start.24 = (s32[1,64,2]{1,2,0:T(2,128)S(1)}, s32[1,64,2]{1,2,0:T(2,128)}, u32[]{:S(2)}) copy-start(s32[1,64,2]{1,2,0:T(2,128)} %param.18) | copy-start | bytes 1540
  7.2 89.3 %all-gather.17.cloned.1.call-start = ((), (), s32[]{:S(2)}) async-start(), calls=%async_computation.3 | async-start | bytes 2162688 | tf_op jit(solution)/shard_map/all_gather | solution.py:12
  15.6 159.2 %all-gather.19.cloned.1.call-start = ((), (), s32[]{:S(2)}) async-start(), calls=%async_computation.4 | async-start | bytes 2162688 | tf_op jit(solution)/shard_map/all_gather | solution.py:12
  16.4 236.8 %all-gather.21.cloned.1.call-start = ((), (), s32[]{:S(2)}) async-start(), calls=%async_computation.5 | async-start | bytes 2162688 | tf_op jit(solution)/shard_map/all_gather | solution.py:12
  17.1 313.6 %all-gather.23.cloned.1.call-start = ((), (), s32[]{:S(2)}) async-start(), calls=%async_computation.6 | async-start | bytes 2162688 | tf_op jit(solution)/shard_map/all_gather | solution.py:12
  17.7 390.6 %all-gather.25.cloned.1.call-start = ((), (), s32[]{:S(2)}) async-start(), calls=%async_computation.7 | async-start | bytes 2162688 | tf_op jit(solution)/shard_map/all_gather | solution.py:12
  18.3 467.6 %all-gather.27.cloned.1.call-start = ((), (), s32[]{:S(2)}) async-start(), calls=%async_computation.8 | async-start | bytes 2162688 | tf_op jit(solution)/shard_map/all_gather | solution.py:12
  18.8 544.8 %all-gather.29.cloned.1.call-start = ((), (), s32[]{:S(2)}) async-start(), calls=%async_computation.9 | async-start | bytes 2162688 | tf_op jit(solution)/shard_map/all_gather | solution.py:12
  19.6 622.3 %all-gather.31.cloned.1.call-start = ((), (), s32[]{:S(2)}) async-start(), calls=%async_computation.10 | async-start | bytes 2162688 | tf_op jit(solution)/shard_map/all_gather | solution.py:12
  23.7 631.5 %all-to-all-start = ((bf16[8,64,256]{2,1,0:T(8,128)(2,1)}), bf16[8,64,256]{2,1,0:T(8,128)(2,1)S(1)}, u32[]{:S(2)}, u32[]{:S(2)}) async-start(bf16[8,64,256]{2,1,0:T(8,128)(2,1)} %bitcast.26), calls=%async_computation | async-start | bytes 524288 | tf_op jit(solution)/shard_map/all_to_all | solution.py:53
  29.2 915.5 %all-reduce.6.cloned.1.call-start = ((), (), s32[]{:S(2)}) async-start(), calls=%async_computation.11 | async-start | bytes 1048576 | tf_op jit(solution)/shard_map/psum | solution.py:75
  655.2 3.2 copy-start.7
  655.2 3.2 copy-start.17
  655.2 3.2 copy-start.25
  677.7 9.2 copy-start.23
  694.7 399.4 %all-reduce.4.cloned.1.call-start = ((), (), s32[]{:S(2)}) async-start(), calls=%async_computation.2 | async-start | bytes 1048576 | tf_op jit(solution)/shard_map/psum | solution.py:91
  699.1 8.4 copy-start.3
  702.7 394.4 %all-to-all-start.1 = ((bf16[8,64,256]{2,1,0:T(8,128)(2,1)}), bf16[8,64,256]{2,1,0:T(8,128)(2,1)S(1)}, u32[]{:S(2)}, u32[]{:S(2)}) async-start(bf16[8,64,256]{2,1,0:T(8,128)(2,1)} %bitcast.40), calls=%async_computation.1 | async-start | bytes 524288 | tf_op jit(solution)/shard_map/all_to_all | solution.py:99
  707.5 386.5 %copy-start.19 = (s32[1,8]{1,0:T(1,128)S(1)}, s32[1,8]{1,0:T(1,128)}, u32[]{:S(2)}) copy-start(s32[1,8]{1,0:T(1,128)} %param.20) | copy-start | bytes 100
  707.5 389.6 %copy-start.22 = (s32[512]{0:T(512)S(1)}, s32[512]{0:T(512)}, u32[]{:S(2)}) copy-start(s32[512]{0:T(512)} %eq.97) | copy-start | bytes 6148
  1095.5 5.1 copy-start.16
  (14 other events, 24.9 us)
Sparse Core Ops, SparseCore 0:
  15.7 80.7 all-gather.16
  99.7 75.1 all-gather.18
  178.0 75.1 all-gather.20
  255.6 75.1 all-gather.22
  333.2 75.1 all-gather.24
  410.7 75.1 all-gather.26
  488.5 75.1 all-gather.28
  566.8 75.1 all-gather.30
  694.8 249.7 all-reduce.5
  947.9 146.1 all-reduce.3
